TPU v7x, 32 devices: a whole 2x2x4 slice. The times are simulated.
32 devices in a mesh: grp: 2 (over x), det: 16 (over z, y, core).
Axes of the slice: x: 2, y: 2, z: 4, core: 2. Of those that a mesh axis runs over, the one named last changes fastest.
Arguments:
- timestream: float32 [2, 1024, 16384], P('grp', 'det'), parts along dimension 0, may hold values from -6 to 6
- gains: float32 [2, 1024], P('grp', 'det'), parts along dimension 0, may hold values from 0.5 to 2
- mode_pattern: float32 [2048, 256], P('grp'), parts along dimension 0, may hold values from -0.375 to 0.375
- mode_weights: float32 [2048, 256], P('grp'), parts along dimension 0, may hold values from -0.1875 to 0.1875
- noise_weight: float32 [2048, 16384], P(('grp', 'det')), parts along dimension 0, may hold values from 0.05 to 1
- block_ids: int32 [2, 1024, 64], P('grp', 'det'), parts along dimension 0, may hold values from 0 to 255
- hits: int32 [2, 1024, 64], P('grp', 'det'), parts along dimension 0, may hold values from 0 to 3
- sky_rows: int32 [512], P('grp'), parts along dimension 0, may hold values from 0 to 255, each once
Outputs:
- filtered: float32 [2, 1024, 16384], P('grp', 'det'), parts along dimension 0
- sky_map: float32 [512, 256], P(('grp', 'det')), parts along dimension 0
There are 2 independent parts, one for each index of `grp`. A program takes and returns all parts, laid end to end along the dimension named above; each array names one. Nothing has to cross between parts.
Inputs may be any that keep to these rules, and one draw needn't show every extreme that they name: `sky_rows`: each row number appears exactly once.
All inputs are finite; a program needn't handle non-finite values.
Results may differ from a plain program's by a relative error of at most 0.000078.
Values sent between devices are 32-bit elements; how exact they have to be, the bound alone decides.
No kernel may reach another device: no remote copies, remote signals or barrier semaphores. Data moves between devices by JAX's collectives and lax.ppermute only.
A program may use at most 128 MiB of HBM per device.

v0:
```python
import math
import jax
import jax.numpy as jnp
from jax import lax
from jax.sharding import PartitionSpec as P

SIDE = 128
PIX = 256


def dft_tables(side):
    first = lax.broadcasted_iota(jnp.int32, (side, side), 0)
    second = lax.broadcasted_iota(jnp.int32, (side, side), 1)
    angle = (first * second % side).astype(jnp.float32) * (2.0 * math.pi / side)
    return (jnp.cos(angle), jnp.sin(angle))


def twiddle_tables(side):
    first = lax.broadcasted_iota(jnp.int32, (side, side), 0)
    second = lax.broadcasted_iota(jnp.int32, (side, side), 1)
    angle = (first * second).astype(jnp.float32) * (2.0 * math.pi / (side * side))
    return (jnp.cos(angle), jnp.sin(angle))


def shards(timestream, gains, mode_pattern, mode_weights, noise_weight, block_ids, hits, sky_rows):
    highest = lax.Precision.HIGHEST
    det_local = timestream.shape[1]
    samples = timestream.shape[2]
    calibrated = timestream / gains[:, :, None]
    slab = lax.all_to_all(calibrated, "det", split_axis=2, concat_axis=1, tiled=True)
    coeff = jnp.einsum("dr,odc->orc", mode_weights, slab, precision=highest)
    corrected = slab - jnp.einsum("dr,orc->odc", mode_pattern, coeff, precision=highest)
    cos_table, sin_table = dft_tables(SIDE)
    twist_cos, twist_sin = twiddle_tables(SIDE)
    spectral_weight = noise_weight.reshape(det_local, SIDE, SIDE)
    slab = lax.all_to_all(corrected, "det", split_axis=1, concat_axis=2, tiled=True)
    items = slab.shape[0]
    signal = slab.reshape(items * det_local, SIDE, SIDE)
    section_real = jnp.einsum("kn,rnm->rkm", cos_table, signal, precision=highest)
    section_imag = -jnp.einsum("kn,rnm->rkm", sin_table, signal, precision=highest)
    turned_real = section_real * twist_cos + section_imag * twist_sin
    turned_imag = section_imag * twist_cos - section_real * twist_sin
    freq_real = jnp.einsum("rkn,nj->rjk", turned_real, cos_table, precision=highest) + jnp.einsum(
        "rkn,nj->rjk", turned_imag, sin_table, precision=highest
    )
    freq_imag = jnp.einsum("rkn,nj->rjk", turned_imag, cos_table, precision=highest) - jnp.einsum(
        "rkn,nj->rjk", turned_real, sin_table, precision=highest
    )
    freq_real = (freq_real.reshape(items, det_local, SIDE, SIDE) * spectral_weight).reshape(
        items * det_local, SIDE, SIDE
    )
    freq_imag = (freq_imag.reshape(items, det_local, SIDE, SIDE) * spectral_weight).reshape(
        items * det_local, SIDE, SIDE
    )
    back_real = jnp.einsum("rjk,jm->rkm", freq_real, cos_table, precision=highest) - jnp.einsum(
        "rjk,jm->rkm", freq_imag, sin_table, precision=highest
    )
    back_imag = jnp.einsum("rjk,jm->rkm", freq_imag, cos_table, precision=highest) + jnp.einsum(
        "rjk,jm->rkm", freq_real, sin_table, precision=highest
    )
    final_real = back_real * twist_cos - back_imag * twist_sin
    final_imag = back_imag * twist_cos + back_real * twist_sin
    result = jnp.einsum("nk,rkm->rnm", cos_table, final_real, precision=highest) - jnp.einsum(
        "nk,rkm->rnm", sin_table, final_imag, precision=highest
    )
    filtered = (result / samples).reshape(items, det_local, samples)
    tile_rows = filtered.reshape(-1, PIX)
    weight = hits.reshape(-1).astype(jnp.float32)
    ids_flat = block_ids.reshape(-1)
    blocks = sky_rows.shape[0]
    ladder = lax.broadcasted_iota(jnp.int32, (blocks, ids_flat.shape[0]), 0)
    rows = jnp.sum(jnp.where(ids_flat[None, :] == ladder, sky_rows[:, None], 0), axis=0)
    table = jnp.where(rows[None, :] == ladder, weight[None, :], 0.0)
    sums = jnp.dot(table, tile_rows, precision=highest, preferred_element_type=jnp.float32)
    counts = jnp.sum(table, axis=1)
    own_sums, own_counts = (
        lax.psum_scatter(sums, "det", scatter_dimension=0, tiled=True),
        lax.psum_scatter(counts, "det", scatter_dimension=0, tiled=True),
    )
    sky_map = own_sums / jnp.sqrt(1.0 + own_counts)[:, None]
    return (filtered, sky_map)


def solution(mesh):
    in_specs = (
        P("grp", "det", None),
        P("grp", "det"),
        P("grp", None),
        P("grp", None),
        P(("grp", "det"), None),
        P("grp", "det", None),
        P("grp", "det", None),
        P("grp"),
    )
    out_specs = (P("grp", "det", None), P(("grp", "det"), None))
    return jax.shard_map(shards, mesh=mesh, in_specs=in_specs, out_specs=out_specs, check_vma=False)
```

profile of v0, /device:TPU:0, one launch (start us, length us, event | category | flops | bytes accessed | tf_op | source)
XLA Modules:
  0.0 547.4 jit_solution(1143022647342395061)
XLA Ops:
  7.2 0.0 copy-start
  7.2 4.7 broadcast_divide_fusion
  11.9 17.1 %copy.141 = f32[1,64,16384]{1,0,2:T(1,128)} copy(f32[1,64,16384]{2,1,0:T(8,128)} %broadcast_divide_fusion) | data formatting | bytes 8388608 | tf_op jit(solution)/shard_map/div | solution.py:29
  29.0 0.5 broadcast.67
  29.5 74.5 %reduce = f32[16384,64]{1,0:T(8,128)} reduce(f32[16384,1,64]{2,1,0:T(1,128)} %bitcast.98, f32[]{:T(128)} %broadcast.67), dimensions={1}, to_apply=%bitcast.83.reduce_sub_computation | reduce | bytes 8388612
  103.9 13.3 %reshape.70 = f32[16,1,65536]{2,1,0:T(1,128)} reshape(f32[16384,64]{1,0:T(8,128)} %reduce) | data formatting | bytes 8388608
  117.2 100.1 %all_to_all.33 = f32[16,1,65536]{2,1,0:T(1,128)} all-to-all(f32[16,1,65536]{2,1,0:T(1,128)} %reshape.70), channel_id=1, replica_groups=mesh['grp'=2,'det'=16] {'det'}, dimensions={0} | all-to-all | bytes 8388608 | tf_op jit(solution)/shard_map/all_to_all | solution.py:30
  217.3 13.8 %reduce.1 = f32[16,65536]{1,0:T(8,128)} reduce(f32[16,1,65536]{2,1,0:T(1,128)} %all_to_all.33, f32[]{:T(128)} %broadcast.67), dimensions={1}, to_apply=%all_to_all.24.reduce_sub_computation | reduce | bytes 8388612 | tf_op jit(solution)/shard_map/all_to_all | solution.py:30
  231.1 14.0 %reshape.71 = f32[16384,1,64]{2,1,0:T(1,128)} reshape(f32[16,65536]{1,0:T(8,128)} %reduce.1) | data formatting | bytes 8388608
  245.1 7.3 %copy.189 = f32[1,64,16,1024]{3,2,1,0:T(8,128)} copy(f32[1,64,16,1024]{1,3,2,0:T(8,128)} %bitcast.99) | data formatting | bytes 8388608 | tf_op jit(solution)/shard_map/all_to_all | solution.py:30
  252.4 6.5 %copy.143 = f32[1,16,64,1024]{3,2,1,0:T(8,128)} copy(f32[1,16,64,1024]{3,1,2,0:T(8,128)} %bitcast.100) | data formatting | bytes 8388608 | tf_op jit(solution)/shard_map/all_to_all | solution.py:30
  258.9 5.4 copy.145
  264.4 0.0 copy-done.5
  264.4 8.8 %convolution_bitcast_fusion = f32[256,1024]{0,1:T(8,128)S(1)} fusion(f32[1024,1024]{1,0:T(8,128)} %bitcast.97, f32[1024,256]{1,0:T(8,128)S(1)} %copy-done.5), kind=kOutput, calls=%fused_computation.34 | convolution fusion | flops 3221225472 | bytes 6291456 | tf_op jit(solution)/shard_map/dr,odc->orc/dot_general | solution.py:31
  273.2 0.0 copy-done
  273.2 0.0 copy-done.4
  273.2 5.2 bitcast_subtract_fusion
  278.4 11.0 %copy.146 = f32[1,1024,1024]{2,0,1:T(1,128)} copy(f32[1,1024,1024]{1,2,0:T(8,128)} %bitcast_subtract_fusion) | data formatting | bytes 8388608 | tf_op jit(solution)/shard_map/sub | solution.py:32
  289.4 5.4 all-to-all-start.1
  294.8 0.0 reduce-scatter.2.cloned.1.call-start
  294.8 0.2 fusion.47
  295.1 0.1 copy.149
  295.2 0.2 fusion.46
  295.4 0.1 copy.151
  295.5 0.0 copy-start.7
  295.5 0.0 copy-start.6
  295.5 0.0 copy-start.8
  295.5 5.0 copy.194
  300.5 0.0 copy-done.7
  300.5 0.1 convert_element_type.62
  300.6 0.0 copy-done.6
  300.6 0.1 eq.20
  300.7 0.0 copy-done.8
  300.7 0.7 select_reduce_fusion.1
  301.4 70.9 %all-to-all-done.1 = f32[1,1024,1024]{2,0,1:T(1,128)} async-done(((f32[1,1024,1024]{2,0,1:T(1,128)}), f32[1,1024,1024]{2,0,1:T(1,128)}, u32[]{:S(2)}, u32[]{:S(2)}) %all-to-all-start.1) | async-done | bytes 4194336 | tf_op jit(solution)/shard_map/all_to_all | solution.py:36
  372.3 3.2 copy.193
  375.5 4.4 copy.147
  379.9 4.9 reshape.61
  384.8 9.5 %fusion.35 = f32[64,128,128]{2,1,0:T(8,128)S(1)} fusion(f32[64,128,128]{2,1,0:T(8,128)} %reshape.61), kind=kOutput, calls=%fused_computation.48 | convolution fusion | flops 1610842112 | bytes 8388608 | tf_op jit(solution)/shard_map/kn,rnm->rkm/dot_general | solution.py:40
  394.3 0.0 copy-done.3
  394.3 7.0 %fusion.43 = f32[64,128,128]{2,1,0:T(8,128)S(1)} fusion(f32[64,128,128]{2,1,0:T(8,128)S(1)} %copy-done.3), kind=kOutput, calls=%fused_computation.56 | convolution fusion | flops 1610842112 | bytes 8388608 | tf_op jit(solution)/shard_map/kn,rnm->rkm/dot_general | solution.py:39
  401.4 4.7 fusion.21
  406.1 0.0 copy-start.2
  406.1 4.8 fusion.25
  410.8 0.0 copy-done.2
  410.9 5.1 bitcast_multiply_fusion
  416.0 4.8 fusion.39
  420.8 5.2 bitcast_multiply_fusion.1
  426.0 4.5 fusion.41
  430.5 5.1 convolution_add_fusion
  435.7 4.7 convolution_subtract_fusion
  440.4 4.1 fusion.4
  444.5 5.7 %multiply_bitcast_fusion = f32[64,128,128]{1,2,0:T(8,128)} fusion(f32[64,128,128]{2,1,0:T(8,128)S(1)} %fusion.4, f32[64,128,128]{1,2,0:T(8,128)S(1)} %convolution_add_fusion, f32[64,128,128]{1,2,0:T(8,128)S(1)} %convolution_subtract_fusion, f32[128,128]{0,1:T(8,128)S(1)} %copy.151, f32[128,128]{0,1:T(8,128)S(1)} %copy.149), kind=kOutput, calls=%fused_computation.15 | convolution fusion | flops 1616084992 | bytes 16908288 | tf_op jit(solution)/shard_map/nk,rkm->rnm/dot_general | solution.py:63
  450.2 5.8 %copy.168 = f32[64,128,128]{2,1,0:T(8,128)} copy(f32[64,128,128]{1,2,0:T(8,128)} %multiply_bitcast_fusion) | data formatting | bytes 8388608 | tf_op jit(solution)/shard_map/div | solution.py:66
  455.9 5.2 reshape_reshape.3
  461.1 6.9 %fusion = f32[256,256]{1,0:T(8,128)} fusion(f32[4096,256]{1,0:T(8,128)} %reshape_reshape.3, f32[4096]{0:T(1024)S(1)} %convert_element_type.62, s32[4096]{0:T(1024)S(1)} %select_reduce_fusion.1), kind=kOutput, calls=%fused_computation.1 | convolution fusion | flops 3223322624 | bytes 4489216 | tf_op jit(solution)/shard_map/dot_general | solution.py:74
  468.0 0.0 reduce-scatter.2.cloned.1.call-update
  468.0 0.6 dynamic-slice
  469.3 0.6 select_reduce_fusion
  469.9 47.8 %all-reduce = f32[256]{0:T(256)S(1)} all-reduce(f32[256]{0:T(256)S(1)} %select_reduce_fusion), channel_id=3, replica_groups=mesh['grp'=2,'det'=16] {'det'}, use_global_device_ids=true, to_apply=%region_3.4.clone | all-reduce | flops 256 | bytes 2048
  517.7 0.1 fusion.65
  517.7 5.0 reshape.62
  522.8 16.2 %reduce-scatter.2.cloned.1.call-done = f32[16,256]{1,0:T(8,128)} async-done(((f32[256,256]{1,0:T(8,128)}), f32[16,256]{1,0:T(8,128)}) %reduce-scatter.2.cloned.1.call-update) | async-done | bytes 16400 | tf_op jit(solution)/shard_map/reduce_scatter | solution.py:77
  538.9 1.4 broadcast_divide_fusion.1
  (8 shorter events, 0.0 us)
Async XLA Ops:
  7.2 266.0 %copy-start = (f32[1024,256]{1,0:T(8,128)S(1)}, f32[1024,256]{1,0:T(8,128)}, u32[]{:S(2)}) copy-start(f32[1024,256]{1,0:T(8,128)} %param.10) | copy-start | bytes 3145732
  258.9 5.4 copy-start.5
  264.4 8.8 %copy-start.4 = (f32[1,1024,1024]{1,2,0:T(8,128)S(1)}, f32[1,1024,1024]{1,2,0:T(8,128)}, u32[]{:S(2)}) copy-start(f32[1,1024,1024]{1,2,0:T(8,128)} %copy.145) | copy-start | bytes 12582916
  289.4 82.9 %all-to-all-start.1 = ((f32[1,1024,1024]{2,0,1:T(1,128)}), f32[1,1024,1024]{2,0,1:T(1,128)}, u32[]{:S(2)}, u32[]{:S(2)}) async-start(f32[1,1024,1024]{2,0,1:T(1,128)} %copy.146), calls=%async_computation.1 | async-start | bytes 8388608 | tf_op jit(solution)/shard_map/all_to_all | solution.py:36
  294.8 244.2 %reduce-scatter.2.cloned.1.call-start = ((), (), s32[]{:S(2)}) async-start(), calls=%async_computation.3 | async-start | bytes 278528 | tf_op jit(solution)/shard_map/reduce_scatter | solution.py:77
  295.5 5.0 copy-start.7
  295.5 5.1 copy-start.6
  295.5 5.1 copy-start.8
  384.8 9.5 %copy-start.3 = (f32[64,128,128]{2,1,0:T(8,128)S(1)}, f32[64,128,128]{2,1,0:T(8,128)}, u32[]{:S(2)}) copy-start(f32[64,128,128]{2,1,0:T(8,128)} %reshape.61) | copy-start | bytes 12582916
  406.1 4.8 copy-start.2
  461.1 6.9 %copy-start.9 = (u32[32]{0:T(128)S(1)}, u32[32]{0:T(128)}, u32[]{:S(2)}) copy-start(u32[32]{0:T(128)} %constant.33) | copy-start | bytes 388
  517.7 22.7 %copy-start.1 = (f32[1024,256]{1,0:T(8,128)S(1)}, f32[1024,256]{1,0:T(8,128)}, u32[]{:S(2)}) copy-start(f32[1024,256]{1,0:T(8,128)} %param.10) | copy-start | bytes 3145732
Sparse Core Ops, SparseCore 0:
  468.1 70.7 reduce-scatter.1
where the time goes:
time: 553 us; the launch traced here: 547 us
  blocking collectives  148 us (27%)
  local copies, waits for them, and re-layouts  109 us (20%)
  other arithmetic  96.2 us (17%)
  waiting for transfers between devices  87.1 us (16%)
  matrix products  86.2 us (16%)
  between operations  15.1 us (3%)
    all_to_all x1, blocking collectives, shards(): lax.all_to_all(calibrated, 'det', split_axis=2, concat_axis=1, tiled=True)  100 us
    unnamed x1, other arithmetic  74.5 us
    all_to_all x1, waiting for transfers between devices, shards(): lax.all_to_all(corrected, 'det', split_axis=1, concat_axis=2, tiled=True)  70.9 us
    unnamed x1, blocking collectives  47.8 us
    unnamed x26, local copies, waits for them, and re-layouts  36.5 us
    all_to_all x3, local copies, waits for them, and re-layouts, shards(): lax.all_to_all(calibrated, 'det', split_axis=2, concat_axis=1, tiled=True)  19.3 us
    div x1, local copies, waits for them, and re-layouts, shards(): calibrated = timestream / gains[:, :, None]  17.1 us
    reduce_scatter x1, waiting for transfers between devices, shards(): lax.psum_scatter(sums, 'det', scatter_dimension=0, tiled=True)  16.2 us
  transfers between devices with their start and end apart: 2, of which 2 were waited for; matrix products, arithmetic and copies ran while one was open for 2% of the time, Pallas kernels for 0%

commit v1 on v0

--- a/solution.py
+++ b/solution.py
@@ -27,7 +27,10 @@
     det_local = timestream.shape[1]
     samples = timestream.shape[2]
     calibrated = timestream / gains[:, :, None]
-    slab = lax.all_to_all(calibrated, "det", split_axis=2, concat_axis=1, tiled=True)
+    slab = jnp.concatenate(
+        lax.all_to_all(jnp.stack(jnp.split(calibrated, lax.axis_size("det"), axis=2)), "det", 0, 0),
+        axis=1,
+    )
     coeff = jnp.einsum("dr,odc->orc", mode_weights, slab, precision=highest)
     corrected = slab - jnp.einsum("dr,orc->odc", mode_pattern, coeff, precision=highest)
     cos_table, sin_table = dft_tables(SIDE)

time: 553 us -> 404 us (0.73)
  other arithmetic: 96.2 us -> 5.93 us
  local copies, waits for them, and re-layouts: 109 us -> 51.1 us
    unnamed x1 -> x0, other arithmetic: 74.5 us -> none
    unnamed x26 -> x38, local copies, waits for them, and re-layouts: 36.5 us -> 9.09 us
    all_to_all x3 -> x0, local copies, waits for them, and re-layouts: 19.3 us -> none  [shards(): lax.all_to_all(calibrated, 'det', split_axis=2, concat_axis=1, tiled=True)]
    div x1 -> x0, local copies, waits for them, and re-layouts: 17.1 us -> none  [shards(): calibrated = timestream / gains[:, :, None]]
    all_to_all x1 -> x0, other arithmetic: 13.8 us -> none  [shards(): lax.all_to_all(calibrated, 'det', split_axis=2, concat_axis=1, tiled=True)]
  transfers between devices with their start and end apart: 2 -> 2, of which waited for: 2 -> 2; matrix products, arithmetic and copies ran while one was open for 2% -> 3% of each run, Pallas kernels for 0% -> 0%
where the time goes in v1:
time: 404 us; the launch traced here: 398 us
  blocking collectives  147 us (36%)
  waiting for transfers between devices  86.8 us (21%)
  matrix products  85.8 us (21%)
  local copies, waits for them, and re-layouts  51.1 us (13%)
  between operations  15.2 us (4%)
  other arithmetic  5.93 us (1%)
  starting transfers between devices  5.72 us (1%)
    all_to_all x1, blocking collectives, shards(): lax.all_to_all(jnp.stack(jnp.split(calibrated, lax.axis_size('det'), axis...  99.4 us
    all_to_all x1, waiting for transfers between devices, shards(): lax.all_to_all(corrected, 'det', split_axis=1, concat_axis=2, tiled=True)  70.6 us
    unnamed x1, blocking collectives  47.8 us
    reduce_scatter x1, waiting for transfers between devices, shards(): lax.psum_scatter(sums, 'det', scatter_dimension=0, tiled=True)  16.2 us
    sub x1, local copies, waits for them, and re-layouts, shards(): slab - jnp.einsum('dr,orc->odc', mode_pattern, coeff, precision=highest)  11 us
    dot_general x1, matrix products, shards(): jnp.einsum('kn,rnm->rkm', sin_table, signal, precision=highest)  9.58 us
    unnamed x38, local copies, waits for them, and re-layouts  9.09 us
    dot_general x1, matrix products, shards(): coeff = jnp.einsum('dr,odc->orc', mode_weights, slab, precision=highest)  8.62 us
  transfers between devices with their start and end apart: 2, of which 2 were waited for; matrix products, arithmetic and copies ran while one was open for 3% of the time, Pallas kernels for 0%

profile of v1, /device:TPU:0, one launch (start us, length us, event | category | flops | bytes accessed | tf_op | source)
XLA Modules:
  0.0 397.8 jit_solution(12811017404580902622)
XLA Ops:
  7.2 0.0 copy-start
  7.2 2.6 broadcast_divide_fusion
  10.3 99.4 %all_to_all.20 = f32[16,1,64,1024]{3,2,1,0:T(8,128)} all-to-all(f32[16,1,64,1024]{3,2,1,0:T(8,128)S(1)} %fusion.27), channel_id=1, replica_groups=mesh['grp'=2,'det'=16] {'det'}, dimensions={0} | all-to-all | bytes 8388608 | tf_op jit(solution)/shard_map/all_to_all | solution.py:31
  109.7 0.0 copy-start.5
  109.7 5.4 %copy.94 = f32[1,1024,1024]{1,2,0:T(8,128)} copy(f32[1,1024,1024]{2,1,0:T(8,128)} %bitcast.156) | data formatting | bytes 8388608 | tf_op jit(solution)/shard_map/reshape | solution.py:30
  115.1 0.0 copy-start.4
  115.1 0.0 copy-done.5
  115.1 8.6 %convolution_bitcast_fusion = f32[256,1024]{0,1:T(8,128)S(1)} fusion(f32[1024,1024]{1,0:T(8,128)} %bitcast.157, f32[1024,256]{1,0:T(8,128)S(1)} %copy-done.5), kind=kOutput, calls=%fused_computation.34 | convolution fusion | flops 3221225472 | bytes 6291456 | tf_op jit(solution)/shard_map/dr,odc->orc/dot_general | solution.py:34
  123.7 0.0 copy-done
  123.7 0.0 copy-done.4
  123.8 5.2 %bitcast_subtract_fusion = f32[1,1024,1024]{1,2,0:T(8,128)} fusion(f32[1,1024,1024]{1,2,0:T(8,128)S(1)} %copy-done.4, f32[256,1024]{0,1:T(8,128)S(1)} %convolution_bitcast_fusion, f32[1024,256]{1,0:T(8,128)S(1)} %copy-done), kind=kOutput, calls=%fused_computation.5 | convolution fusion | flops 3222274048 | bytes 10485760 | tf_op jit(solution)/shard_map/dr,orc->odc/dot_general | solution.py:35
  129.0 11.0 %copy.95 = f32[1,1024,1024]{2,0,1:T(1,128)} copy(f32[1,1024,1024]{1,2,0:T(8,128)} %bitcast_subtract_fusion) | data formatting | bytes 8388608 | tf_op jit(solution)/shard_map/sub | solution.py:35
  140.0 5.4 %all-to-all-start.1 = ((f32[1,1024,1024]{2,0,1:T(1,128)}), f32[1,1024,1024]{2,0,1:T(1,128)}, u32[]{:S(2)}, u32[]{:S(2)}) async-start(f32[1,1024,1024]{2,0,1:T(1,128)} %copy.95), calls=%async_computation.1 | async-start | bytes 8388608 | tf_op jit(solution)/shard_map/all_to_all | solution.py:39
  145.4 0.3 reduce-scatter.2.cloned.1.call-start
  145.7 0.2 fusion.62
  145.9 0.1 copy.100
  146.0 0.2 fusion.63
  146.3 0.1 copy.98
  146.4 0.0 copy-start.7
  146.4 0.0 copy-start.6
  146.4 0.0 copy-start.8
  146.4 5.0 %copy.142 = f32[8,8,128,128]{3,2,1,0:T(8,128)} copy(f32[8,8,128,128]{3,1,2,0:T(8,128)} %bitcast.159) | data formatting | bytes 8388608
  151.4 0.0 copy-done.7
  151.4 0.1 convert_element_type.62
  151.4 0.0 copy-done.6
  151.5 0.1 eq.20
  151.5 0.0 copy-done.8
  151.5 0.7 select_reduce_fusion.1
  152.3 70.6 %all-to-all-done.1 = f32[1,1024,1024]{2,0,1:T(1,128)} async-done(((f32[1,1024,1024]{2,0,1:T(1,128)}), f32[1,1024,1024]{2,0,1:T(1,128)}, u32[]{:S(2)}, u32[]{:S(2)}) %all-to-all-start.1) | async-done | bytes 4194336 | tf_op jit(solution)/shard_map/all_to_all | solution.py:39
  222.9 3.2 copy.141
  226.1 4.4 %copy.96 = f32[1,64,16,1024]{3,2,1,0:T(8,128)} copy(f32[1,64,16,1024]{3,1,2,0:T(8,128)S(1)} %bitcast.158) | data formatting | bytes 8388608 | tf_op jit(solution)/shard_map/all_to_all | solution.py:39
  230.5 4.9 %reshape.65 = f32[64,128,128]{2,1,0:T(8,128)} reshape(f32[1,64,16,1024]{3,2,1,0:T(8,128)} %copy.96) | data formatting | bytes 8388608 | tf_op jit(solution)/shard_map/reshape | solution.py:41
  235.4 0.0 copy-start.3
  235.4 9.6 %fusion.51 = f32[64,128,128]{2,1,0:T(8,128)S(1)} fusion(f32[64,128,128]{2,1,0:T(8,128)} %reshape.65), kind=kOutput, calls=%fused_computation.80 | convolution fusion | flops 1610842112 | bytes 8388608 | tf_op jit(solution)/shard_map/kn,rnm->rkm/dot_general | solution.py:43
  245.0 0.0 copy-done.3
  245.0 7.0 %fusion.59 = f32[64,128,128]{2,1,0:T(8,128)S(1)} fusion(f32[64,128,128]{2,1,0:T(8,128)S(1)} %copy-done.3), kind=kOutput, calls=%fused_computation.88 | convolution fusion | flops 1610842112 | bytes 8388608 | tf_op jit(solution)/shard_map/kn,rnm->rkm/dot_general | solution.py:42
  252.0 4.7 %fusion.21 = f32[128,64,128]{2,0,1:T(8,128)S(1)} fusion(f32[64,128,128]{2,1,0:T(8,128)S(1)} %fusion.59, f32[64,128,128]{2,1,0:T(8,128)S(1)} %fusion.51, f32[128,128]{0,1:T(8,128)S(1)} %copy.100, f32[128,128]{0,1:T(8,128)S(1)} %copy.98), kind=kOutput, calls=%fused_computation.35 | convolution fusion | flops 1615036416 | bytes 12713984 | tf_op jit(solution)/shard_map/rkn,nj->rjk/dot_general | solution.py:49
  256.7 0.0 copy-start.2
  256.7 4.8 %fusion.25 = f32[128,64,128]{2,0,1:T(8,128)S(1)} fusion(f32[64,128,128]{2,1,0:T(8,128)S(1)} %fusion.59, f32[64,128,128]{2,1,0:T(8,128)S(1)} %fusion.51, f32[128,128]{0,1:T(8,128)S(1)} %copy.100, f32[128,128]{0,1:T(8,128)S(1)} %copy.98), kind=kOutput, calls=%fused_computation.36 | convolution fusion | flops 1615036416 | bytes 12713984 | tf_op jit(solution)/shard_map/rkn,nj->rjk/dot_general | solution.py:46
  261.5 0.0 copy-done.2
  261.5 5.1 %bitcast_multiply_fusion = f32[64,128,128]{2,1,0:T(8,128)S(1)} fusion(f32[8,8,128,128]{3,2,1,0:T(8,128)S(1)} %copy-done.2, f32[128,64,128]{2,0,1:T(8,128)S(1)} %fusion.21, f32[64,128,128]{2,1,0:T(8,128)S(1)} %fusion.59, f32[64,128,128]{2,1,0:T(8,128)S(1)} %fusion.51, f32[128,128]{0,1:T(8,128)S(1)} %copy.100, f32[128,128]{0,1:T(8,128)S(1)} %copy.98), kind=kOutput, calls=%fused_computation.3 | convolution fusion | flops 1617133568 | bytes 21102592 | tf_op jit(solution)/shard_map/rkn,nj->rjk/dot_general | solution.py:49
  266.6 4.8 %fusion.55 = f32[64,128,128]{1,2,0:T(8,128)S(1)} fusion(f32[64,128,128]{2,1,0:T(8,128)S(1)} %bitcast_multiply_fusion), kind=kOutput, calls=%fused_computation.84 | convolution fusion | flops 1610842112 | bytes 8388608 | tf_op jit(solution)/shard_map/rjk,jm->rkm/dot_general | solution.py:61
  271.4 5.2 %bitcast_multiply_fusion.1 = f32[64,128,128]{2,1,0:T(8,128)S(1)} fusion(f32[8,8,128,128]{3,2,1,0:T(8,128)S(1)} %copy-done.2, f32[128,64,128]{2,0,1:T(8,128)S(1)} %fusion.25, f32[64,128,128]{2,1,0:T(8,128)S(1)} %fusion.59, f32[64,128,128]{2,1,0:T(8,128)S(1)} %fusion.51, f32[128,128]{0,1:T(8,128)S(1)} %copy.100, f32[128,128]{0,1:T(8,128)S(1)} %copy.98), kind=kOutput, calls=%fused_computation.4 | convolution fusion | flops 1617133568 | bytes 21102592 | tf_op jit(solution)/shard_map/rkn,nj->rjk/dot_general | solution.py:46
  276.6 4.5 %fusion.57 = f32[64,128,128]{1,2,0:T(8,128)S(1)} fusion(f32[64,128,128]{2,1,0:T(8,128)S(1)} %bitcast_multiply_fusion.1), kind=kOutput, calls=%fused_computation.86 | convolution fusion | flops 1610842112 | bytes 8388608 | tf_op jit(solution)/shard_map/rjk,jm->rkm/dot_general | solution.py:58
  281.1 5.1 %convolution_add_fusion = f32[64,128,128]{1,2,0:T(8,128)S(1)} fusion(f32[64,128,128]{1,2,0:T(8,128)S(1)} %fusion.55, f32[64,128,128]{2,1,0:T(8,128)S(1)} %bitcast_multiply_fusion.1), kind=kOutput, calls=%fused_computation.24 | convolution fusion | flops 1611890688 | bytes 12582912 | tf_op jit(solution)/shard_map/rjk,jm->rkm/dot_general | solution.py:61
  286.3 4.5 %convolution_subtract_fusion = f32[64,128,128]{1,2,0:T(8,128)S(1)} fusion(f32[64,128,128]{1,2,0:T(8,128)S(1)} %fusion.57, f32[64,128,128]{2,1,0:T(8,128)S(1)} %bitcast_multiply_fusion), kind=kOutput, calls=%fused_computation.25 | convolution fusion | flops 1611890688 | bytes 12582912 | tf_op jit(solution)/shard_map/rjk,jm->rkm/dot_general | solution.py:58
  290.8 4.1 %fusion.4 = f32[64,128,128]{2,1,0:T(8,128)S(1)} fusion(f32[64,128,128]{1,2,0:T(8,128)S(1)} %convolution_subtract_fusion, f32[64,128,128]{1,2,0:T(8,128)S(1)} %convolution_add_fusion, f32[128,128]{0,1:T(8,128)S(1)} %copy.100, f32[128,128]{0,1:T(8,128)S(1)} %copy.98), kind=kOutput, calls=%fused_computation.16 | convolution fusion | flops 1613987840 | bytes 12713984 | tf_op jit(solution)/shard_map/nk,rkm->rnm/dot_general | solution.py:66
  294.9 5.7 %multiply_bitcast_fusion = f32[64,128,128]{1,2,0:T(8,128)} fusion(f32[64,128,128]{2,1,0:T(8,128)S(1)} %fusion.4, f32[64,128,128]{1,2,0:T(8,128)S(1)} %convolution_add_fusion, f32[64,128,128]{1,2,0:T(8,128)S(1)} %convolution_subtract_fusion, f32[128,128]{0,1:T(8,128)S(1)} %copy.100, f32[128,128]{0,1:T(8,128)S(1)} %copy.98), kind=kOutput, calls=%fused_computation.15 | convolution fusion | flops 1616084992 | bytes 16908288 | tf_op jit(solution)/shard_map/nk,rkm->rnm/dot_general | solution.py:66
  300.6 5.8 %copy.117 = f32[64,128,128]{2,1,0:T(8,128)} copy(f32[64,128,128]{1,2,0:T(8,128)} %multiply_bitcast_fusion) | data formatting | bytes 8388608 | tf_op jit(solution)/shard_map/div | solution.py:69
  306.3 5.2 %reshape_reshape.3 = f32[4096,256]{1,0:T(8,128)} reshape(f32[64,128,128]{2,1,0:T(8,128)} %copy.117) | data formatting | bytes 8388608 | tf_op jit(solution)/shard_map/reshape;reshape | solution.py:70
  311.5 0.0 copy-start.9
  311.5 6.9 %fusion = f32[256,256]{1,0:T(8,128)} fusion(f32[4096,256]{1,0:T(8,128)} %reshape_reshape.3, f32[4096]{0:T(1024)S(1)} %convert_element_type.62, s32[4096]{0:T(1024)S(1)} %select_reduce_fusion.1), kind=kOutput, calls=%fused_computation.1 | convolution fusion | flops 3223322624 | bytes 4489216 | tf_op jit(solution)/shard_map/dot_general | solution.py:77
  318.4 0.0 reduce-scatter.2.cloned.1.call-update
  318.4 0.0 copy-done.9
  318.4 0.6 dynamic-slice
  319.7 0.6 select_reduce_fusion
  320.3 47.8 %all-reduce = f32[256]{0:T(256)S(1)} all-reduce(f32[256]{0:T(256)S(1)} %select_reduce_fusion), channel_id=3, replica_groups=mesh['grp'=2,'det'=16] {'det'}, use_global_device_ids=true, to_apply=%region_3.4.clone | all-reduce | flops 256 | bytes 2048
  368.1 0.0 copy-start.1
  368.1 0.1 fusion.81
  368.1 5.0 %reshape.66 = f32[1,64,16384]{2,1,0:T(8,128)} reshape(f32[64,128,128]{2,1,0:T(8,128)} %copy.117) | data formatting | bytes 8388608 | tf_op jit(solution)/shard_map/reshape | solution.py:69
  373.2 16.2 %reduce-scatter.2.cloned.1.call-done = f32[16,256]{1,0:T(8,128)} async-done(((f32[256,256]{1,0:T(8,128)}), f32[16,256]{1,0:T(8,128)}) %reduce-scatter.2.cloned.1.call-update) | async-done | bytes 16400 | tf_op jit(solution)/shard_map/reduce_scatter | solution.py:80
  389.3 1.4 broadcast_divide_fusion.1
  390.7 0.0 copy-done.1
  (17 shorter events, 0.3 us)
Async XLA Ops:
  7.2 116.6 %copy-start = (f32[1024,256]{1,0:T(8,128)S(1)}, f32[1024,256]{1,0:T(8,128)}, u32[]{:S(2)}) copy-start(f32[1024,256]{1,0:T(8,128)} %param.10) | copy-start | bytes 3145732
  109.7 5.4 %copy-start.5 = (f32[1024,256]{1,0:T(8,128)S(1)}, f32[1024,256]{1,0:T(8,128)}, u32[]{:S(2)}) copy-start(f32[1024,256]{1,0:T(8,128)} %param.11) | copy-start | bytes 3145732
  115.1 8.6 %copy-start.4 = (f32[1,1024,1024]{1,2,0:T(8,128)S(1)}, f32[1,1024,1024]{1,2,0:T(8,128)}, u32[]{:S(2)}) copy-start(f32[1,1024,1024]{1,2,0:T(8,128)} %copy.94) | copy-start | bytes 12582916
  140.0 82.9 %all-to-all-start.1 = ((f32[1,1024,1024]{2,0,1:T(1,128)}), f32[1,1024,1024]{2,0,1:T(1,128)}, u32[]{:S(2)}, u32[]{:S(2)}) async-start(f32[1,1024,1024]{2,0,1:T(1,128)} %copy.95), calls=%async_computation.1 | async-start | bytes 8388608 | tf_op jit(solution)/shard_map/all_to_all | solution.py:39
  145.4 244.0 %reduce-scatter.2.cloned.1.call-start = ((), (), s32[]{:S(2)}) async-start(), calls=%async_computation.3 | async-start | bytes 278528 | tf_op jit(solution)/shard_map/reduce_scatter | solution.py:80
  146.4 5.0 %copy-start.7 = (s32[1,64,64]{2,1,0:T(8,128)S(1)}, s32[1,64,64]{2,1,0:T(8,128)}, u32[]{:S(2)}) copy-start(s32[1,64,64]{2,1,0:T(8,128)} %param.14) | copy-start | bytes 49156
  146.4 5.1 %copy-start.6 = (s32[1,64,64]{2,1,0:T(8,128)S(1)}, s32[1,64,64]{2,1,0:T(8,128)}, u32[]{:S(2)}) copy-start(s32[1,64,64]{2,1,0:T(8,128)} %param.13) | copy-start | bytes 49156
  146.4 5.1 %copy-start.8 = (s32[256]{0:T(256)S(1)}, s32[256]{0:T(256)}, u32[]{:S(2)}) copy-start(s32[256]{0:T(256)} %param.15) | copy-start | bytes 3076
  235.4 9.6 %copy-start.3 = (f32[64,128,128]{2,1,0:T(8,128)S(1)}, f32[64,128,128]{2,1,0:T(8,128)}, u32[]{:S(2)}) copy-start(f32[64,128,128]{2,1,0:T(8,128)} %reshape.65) | copy-start | bytes 12582916
  256.7 4.8 %copy-start.2 = (f32[8,8,128,128]{3,2,1,0:T(8,128)S(1)}, f32[8,8,128,128]{3,2,1,0:T(8,128)}, u32[]{:S(2)}) copy-start(f32[8,8,128,128]{3,2,1,0:T(8,128)} %copy.142) | copy-start | bytes 12582916
  311.5 6.9 %copy-start.9 = (u32[32]{0:T(128)S(1)}, u32[32]{0:T(128)}, u32[]{:S(2)}) copy-start(u32[32]{0:T(128)} %constant.33) | copy-start | bytes 388
  368.1 22.7 %copy-start.1 = (f32[1024,256]{1,0:T(8,128)S(1)}, f32[1024,256]{1,0:T(8,128)}, u32[]{:S(2)}) copy-start(f32[1024,256]{1,0:T(8,128)} %param.10) | copy-start | bytes 3145732
Sparse Core Ops, SparseCore 0:
  318.6 70.7 reduce-scatter.1
